TPU v7x, 32 devices: a whole 2x2x4 slice. The times are simulated.
32 devices in a mesh: gx: 4 (over z), gy: 4 (over x, core), gz: 2 (over y).
Axes of the slice: x: 2, y: 2, z: 4, core: 2. Of those that a mesh axis runs over, the one named last changes fastest.
Arguments:
- activations: bfloat16 [1024, 8192], P('gy', 'gx'), may hold values from -0.5 to 0.5
- cotangent: bfloat16 [1024, 8192], P('gy', 'gx'), may hold values from -1.5 to 1.5
- gate_pre: bfloat16 [1024, 26624], P('gx', ('gy', 'gz')), may hold values from -6 to 6
- up_pre: bfloat16 [1024, 26624], P('gx', ('gy', 'gz')), may hold values from -6 to 6
- gate_weight: bfloat16 [8192, 26624], P('gx', ('gy', 'gz')), may hold values from -0.0625 to 0.0625
- up_weight: bfloat16 [8192, 26624], P('gx', ('gy', 'gz')), may hold values from -0.0625 to 0.0625
- down_weight: bfloat16 [26624, 8192], P(('gy', 'gz'), 'gx'), may hold values from -0.15625 to 0.15625
Outputs:
- input_grad: bfloat16 [1024, 8192], P('gy', 'gx')
- gate_grad: bfloat16 [8192, 26624], P('gx', ('gy', 'gz'))
- up_grad: bfloat16 [8192, 26624], P('gx', ('gy', 'gz'))
- down_grad: bfloat16 [26624, 8192], P(('gy', 'gz'), 'gx')
All inputs are finite; a program needn't handle non-finite values.
Results may differ from a plain program's by a relative error of at most 0.015.
Values may be sent and summed in bfloat16 or wider, within the bound.
A program may use at most 192 MiB of HBM per device.

v0:
```python
import jax
import jax.numpy as jnp
from jax import lax
from jax.sharding import PartitionSpec as P

over_rows = (((0,), (0,)), ((), ()))
over_cols = (((1,), (1,)), ((), ()))


def swiglu_grads(gate_in, up_in, grad_hidden):
    gate_val = gate_in.astype(jnp.float32)
    up_val = up_in.astype(jnp.float32)
    sigmoid = jax.nn.sigmoid(gate_val)
    hidden = (gate_val * sigmoid * up_val).astype(jnp.bfloat16)
    grad_gate = (grad_hidden * up_val * sigmoid * (1.0 + gate_val * (1.0 - sigmoid))).astype(
        jnp.bfloat16
    )
    grad_up = (grad_hidden * gate_val * sigmoid).astype(jnp.bfloat16)
    return (hidden, grad_gate, grad_up)


def input_terms(grad_gate, grad_up, gate_weight, up_weight):

    def compute(offset, amount):
        total = lax.dot_general(
            grad_gate, gate_weight, over_cols, preferred_element_type=jnp.float32
        )
        return total + lax.dot_general(
            grad_up, up_weight, over_cols, preferred_element_type=jnp.float32
        )

    return compute


def shards(activations, cotangent, gate_pre, up_pre, gate_weight, up_weight, down_weight):
    cotangent_all = lax.all_gather(cotangent, "gy", axis=0, tiled=True)
    gate_all, up_all = (
        lax.all_gather(gate_pre, "gx", axis=0, tiled=True),
        lax.all_gather(up_pre, "gx", axis=0, tiled=True),
    )
    local_sum = lax.dot_general(
        cotangent_all, down_weight, over_cols, preferred_element_type=jnp.float32
    )
    grad_hidden = lax.psum(local_sum, "gx")
    hidden, grad_gate, grad_up = swiglu_grads(gate_all, up_all, grad_hidden)
    down_grad = lax.dot_general(
        hidden, cotangent_all, over_rows, preferred_element_type=jnp.float32
    ).astype(jnp.bfloat16)
    segment = lax.all_gather(activations, "gy", axis=0, tiled=True)
    first = lax.dot_general(segment, grad_gate, over_rows, preferred_element_type=jnp.float32)
    second = lax.dot_general(segment, grad_up, over_rows, preferred_element_type=jnp.float32)
    row_count = activations.shape[0]
    terms = input_terms(grad_gate, grad_up, gate_weight, up_weight)
    share_rows = row_count // lax.axis_size("gz")
    input_share = lax.psum_scatter(
        terms(jnp.int32(0), lax.axis_size(("gy", "gz")) * share_rows),
        ("gy", "gz"),
        scatter_dimension=0,
        tiled=True,
    )
    input_grad = lax.all_gather(input_share.astype(jnp.bfloat16), "gz", axis=0, tiled=True)
    return (input_grad, first.astype(jnp.bfloat16), second.astype(jnp.bfloat16), down_grad)


def solution(mesh):
    in_specs = (
        P("gy", "gx"),
        P("gy", "gx"),
        P("gx", ("gy", "gz")),
        P("gx", ("gy", "gz")),
        P("gx", ("gy", "gz")),
        P("gx", ("gy", "gz")),
        P(("gy", "gz"), "gx"),
    )
    out_specs = (P("gy", "gx"), P("gx", ("gy", "gz")), P("gx", ("gy", "gz")), P(("gy", "gz"), "gx"))
    return jax.shard_map(shards, mesh=mesh, in_specs=in_specs, out_specs=out_specs, check_vma=False)
```

profile of v0, /device:TPU:0, one launch (start us, length us, event | category | flops | bytes accessed | tf_op | source)
XLA Modules:
  0.0 951.3 jit_solution(15693381875679629747)
XLA Ops:
  7.2 0.7 all-gather.6.cloned.1.call-update
  7.9 0.7 all-gather.10.cloned.1.call-update
  8.7 0.7 all-gather.8.cloned.1.call-update
  9.4 37.3 %all-gather.6.cloned.1.call-done = bf16[1024,2048]{1,0:T(8,128)(2,1)} async-done(((bf16[256,2048]{1,0:T(8,128)(2,1)}), bf16[1024,2048]{1,0:T(8,128)(2,1)}) %all-gather.6.cloned.1.call-update) | async-done | bytes 4194320 | tf_op jit(solution)/shard_map/all_gather | solution.py:36
  46.8 22.5 %fusion.17 = f32[1024,3328]{1,0:T(8,128)} fusion(bf16[1024,2048]{1,0:T(8,128)(2,1)} %all-gather.6.cloned.1.call-done, bf16[3328,2048]{1,0:T(8,128)(2,1)} %param.13), kind=kOutput, calls=%fused_computation.24 | convolution fusion | flops 13958643712 | bytes 31457280 | tf_op jit(solution)/shard_map/dot_general | solution.py:41
  69.3 0.0 all-gather.14.cloned.1.call-start
  69.4 0.5 all-gather.14.cloned.1.call-update
  69.9 0.2 reduce-scatter.2.cloned.1.call-start
  70.2 102.1 %all-gather.10.cloned.1.call-done = bf16[1024,3328]{1,0:T(8,128)(2,1)} async-done(((bf16[256,3328]{1,0:T(8,128)(2,1)}), bf16[1024,3328]{1,0:T(8,128)(2,1)}) %all-gather.10.cloned.1.call-update) | async-done | bytes 6815760 | tf_op jit(solution)/shard_map/all_gather | solution.py:38
  172.3 123.8 %all-gather.8.cloned.1.call-done = bf16[1024,3328]{1,0:T(8,128)(2,1)} async-done(((bf16[256,3328]{1,0:T(8,128)(2,1)}), bf16[1024,3328]{1,0:T(8,128)(2,1)}) %all-gather.8.cloned.1.call-update) | async-done | bytes 6815760 | tf_op jit(solution)/shard_map/all_gather | solution.py:39
  296.1 461.1 %all-reduce.2.cloned.1.call-done = f32[1024,3328]{1,0:T(8,128)} async-done(((f32[1024,3328]{1,0:T(8,128)}), f32[1024,3328]{1,0:T(8,128)}) %all-reduce.2.cloned.1.call-update) | async-done | bytes 13631504 | tf_op jit(solution)/shard_map/psum | solution.py:44
  757.1 12.2 %fusion.2 = bf16[1024,3328]{1,0:T(8,128)(2,1)S(1)} fusion(f32[1024,3328]{1,0:T(8,128)} %all-reduce.2.cloned.1.call-done, bf16[1024,3328]{1,0:T(8,128)(2,1)} %all-gather.8.cloned.1.call-done, bf16[1024,3328]{1,0:T(8,128)(2,1)} %all-gather.10.cloned.1.call-done), kind=kLoop, calls=%fused_computation.11 | loop fusion | flops 40894464 | bytes 34078720 | tf_op jit(solution)/shard_map/convert_element_type | solution.py:15
  769.3 2.9 copy-done
  772.2 18.1 %fusion.18 = f32[1024,2048]{1,0:T(8,128)} fusion(bf16[1024,3328]{1,0:T(8,128)(2,1)S(1)} %fusion.2, bf16[2048,3328]{1,0:T(8,128)(2,1)} %param.11), kind=kOutput, calls=%fused_computation.25 | convolution fusion | flops 13958643712 | bytes 28835840 | tf_op jit(solution)/shard_map/dot_general | solution.py:25
  790.3 24.1 %convolution_add_fusion = f32[1024,2048]{1,0:T(8,128)} fusion(f32[1024,2048]{1,0:T(8,128)} %fusion.18, bf16[2048,3328]{1,0:T(8,128)(2,1)} %param.12, f32[1024,3328]{1,0:T(8,128)} %all-reduce.2.cloned.1.call-done, bf16[1024,3328]{1,0:T(8,128)(2,1)} %all-gather.10.cloned.1.call-done), kind=kOutput, calls=%fused_computation.22 | convolution fusion | flops 13984595968 | bytes 50855936 | tf_op jit(solution)/shard_map/dot_general | solution.py:28
  814.4 0.3 all-gather.12.cloned.1.call-start
  814.7 23.9 %convolution_convert_fusion = bf16[3328,2048]{1,0:T(8,128)(2,1)} fusion(bf16[1024,2048]{1,0:T(8,128)(2,1)} %all-gather.6.cloned.1.call-done, bf16[1024,3328]{1,0:T(8,128)(2,1)} %all-gather.8.cloned.1.call-done, bf16[1024,3328]{1,0:T(8,128)(2,1)} %all-gather.10.cloned.1.call-done), kind=kOutput, calls=%fused_computation.6 | convolution fusion | flops 13992722432 | bytes 31457280 | tf_op jit(solution)/shard_map/dot_general | solution.py:46
  838.6 23.5 %fusion.11 = bf16[2048,3328]{0,1:T(8,128)(2,1)} fusion(bf16[1024,2048]{1,0:T(8,128)(2,1)} %all-gather.14.cloned.1.call-done, f32[1024,3328]{1,0:T(8,128)} %all-reduce.2.cloned.1.call-done, bf16[1024,3328]{1,0:T(8,128)(2,1)} %all-gather.10.cloned.1.call-done), kind=kOutput, calls=%fused_computation.20 | convolution fusion | flops 13989314560 | bytes 38273024 | tf_op jit(solution)/shard_map/dot_general | solution.py:51
  862.1 22.0 %reduce-scatter.2.cloned.1.call-done = f32[128,2048]{1,0:T(8,128)} async-done(((f32[1024,2048]{1,0:T(8,128)}), f32[128,2048]{1,0:T(8,128)}) %reduce-scatter.2.cloned.1.call-update) | async-done | bytes 1048592 | tf_op jit(solution)/shard_map/reduce_scatter | solution.py:55
  884.1 2.1 convert_element_type.37
  886.2 21.0 %fusion.10 = bf16[2048,3328]{0,1:T(8,128)(2,1)} fusion(bf16[1024,3328]{1,0:T(8,128)(2,1)} %copy-done, bf16[1024,2048]{1,0:T(8,128)(2,1)} %all-gather.14.cloned.1.call-done), kind=kOutput, calls=%fused_computation.19 | convolution fusion | flops 13965459456 | bytes 24641536 | tf_op jit(solution)/shard_map/dot_general | solution.py:50
  907.3 17.4 %copy.11 = bf16[2048,3328]{1,0:T(8,128)(2,1)} copy(bf16[2048,3328]{0,1:T(8,128)(2,1)} %fusion.10) | data formatting | bytes 27262976
  924.7 17.4 %copy.12 = bf16[2048,3328]{1,0:T(8,128)(2,1)} copy(bf16[2048,3328]{0,1:T(8,128)(2,1)} %fusion.11) | data formatting | bytes 27262976
  942.2 2.3 copy.15
  (10 shorter events, 0.2 us)
Async XLA Ops:
  7.2 39.6 %all-gather.6.cloned.1.call-start = ((), (), s32[]{:S(2)}) async-start(), calls=%async_computation.1 | async-start | bytes 5242880 | tf_op jit(solution)/shard_map/all_gather | solution.py:36
  7.9 164.4 %all-gather.10.cloned.1.call-start = ((), (), s32[]{:S(2)}) async-start(), calls=%async_computation.4 | async-start | bytes 8519680 | tf_op jit(solution)/shard_map/all_gather | solution.py:38
  8.6 287.4 %all-gather.8.cloned.1.call-start = ((), (), s32[]{:S(2)}) async-start(), calls=%async_computation.3 | async-start | bytes 8519680 | tf_op jit(solution)/shard_map/all_gather | solution.py:39
  9.4 747.8 %all-reduce.2.cloned.1.call-start = ((), (), s32[]{:S(2)}) async-start(), calls=%async_computation.2 | async-start | bytes 27262976 | tf_op jit(solution)/shard_map/psum | solution.py:44
  69.3 769.3 %all-gather.14.cloned.1.call-start = ((), (), s32[]{:S(2)}) async-start(), calls=%async_computation.7 | async-start | bytes 5242880 | tf_op jit(solution)/shard_map/all_gather | solution.py:49
  69.9 814.2 %reduce-scatter.2.cloned.1.call-start = ((), (), s32[]{:S(2)}) async-start(), calls=%async_computation.5 | async-start | bytes 9437184 | tf_op jit(solution)/shard_map/reduce_scatter | solution.py:55
  769.3 2.9 copy-start
  814.4 127.7 %all-gather.12.cloned.1.call-start = ((), (), s32[]{:S(2)}) async-start(), calls=%async_computation.6 | async-start | bytes 1572864 | tf_op jit(solution)/shard_map/all_gather | solution.py:61
Sparse Core Ops, SparseCore 0:
  9.6 37.1 all-gather.5
  48.3 123.9 all-gather.9
  173.9 122.1 all-gather.7
  299.0 458.1 all-reduce.1
  758.6 33.3 all-gather.13
  814.6 69.5 reduce-scatter.1
  886.4 21.2 all-gather.11
where the time goes:
time: 952 us; the launch traced here: 951 us
  waiting for transfers between devices  749 us (79%)
  matrix products  133 us (14%)
  local copies, waits for them, and re-layouts  40.1 us (4%)
  other arithmetic  14.3 us (2%)
  between operations  14.1 us (1%)
    psum x1, waiting for transfers between devices, shards(): grad_hidden = lax.psum(local_sum, 'gx')  461 us
    all_gather x1, waiting for transfers between devices, shards(): lax.all_gather(up_pre, 'gx', axis=0, tiled=True)  124 us
    all_gather x1, waiting for transfers between devices, shards(): lax.all_gather(gate_pre, 'gx', axis=0, tiled=True)  102 us
    unnamed x5, local copies, waits for them, and re-layouts  40.1 us
    all_gather x1, waiting for transfers between devices, shards(): cotangent_all = lax.all_gather(cotangent, 'gy', axis=0, tiled=True)  37.3 us
    dot_general x1, matrix products, compute(): lax.dot_general(grad_up, up_weight, over_cols, preferred_element_type=jnp...  24.1 us
    dot_general x1, matrix products, shards(): lax.dot_general(hidden, cotangent_all, over_rows, preferred_element_type=...  23.9 us
    dot_general x1, matrix products, shards(): lax.dot_general(segment, grad_up, over_rows, preferred_element_type=jnp.f...  23.5 us
  transfers between devices with their start and end apart: 7, of which 5 were waited for; matrix products, arithmetic and copies ran while one was open for 19% of the time, Pallas kernels for 0%

commit v1 on v0

--- a/solution.py
+++ b/solution.py
@@ -41,7 +41,11 @@
     local_sum = lax.dot_general(
         cotangent_all, down_weight, over_cols, preferred_element_type=jnp.float32
     )
-    grad_hidden = lax.psum(local_sum, "gx")
+    grad_hidden = local_sum
+    for hop in (1, 2):
+        grad_hidden = grad_hidden + lax.ppermute(
+            grad_hidden, "gx", [(dev, dev ^ hop) for dev in range(4)]
+        )
     hidden, grad_gate, grad_up = swiglu_grads(gate_all, up_all, grad_hidden)
     down_grad = lax.dot_general(
         hidden, cotangent_all, over_rows, preferred_element_type=jnp.float32

time: 952 us -> 1390 us (1.46)
  waiting for transfers between devices: 749 us -> 1160 us
  other arithmetic: 14.3 us -> 34.1 us
    ppermute x0 -> x2, waiting for transfers between devices: none -> 639 us  [shards(): lax.ppermute(grad_hidden, 'gx', [(dev, dev ^ hop) for dev in range(4)])]
    psum x1 -> x0, waiting for transfers between devices: 461 us -> none  [shards(): grad_hidden = lax.psum(local_sum, 'gx')]
    all_gather x1, waiting for transfers between devices: 124 us -> 458 us  [shards(): lax.all_gather(up_pre, 'gx', axis=0, tiled=True)]
    all_gather x1, waiting for transfers between devices: 102 us -> 0.03 us  [shards(): lax.all_gather(gate_pre, 'gx', axis=0, tiled=True)]
    add x0 -> x1, other arithmetic: none -> 14.9 us  [shards(): grad_hidden + lax.ppermute(grad_hidden, 'gx', [(dev, dev ^ hop) for dev i...]
  transfers between devices with their start and end apart: 7 -> 8, of which waited for: 5 -> 5; matrix products, arithmetic and copies ran while one was open for 19% -> 13% of each run, Pallas kernels for 0% -> 0%
where the time goes in v1:
time: 1390 us
  waiting for transfers between devices  1160 us (83%)
  matrix products  132 us (9%)
  local copies, waits for them, and re-layouts  37.2 us (3%)
  other arithmetic  34.1 us (2%)
  between operations  15.7 us (1%)
    ppermute x2, waiting for transfers between devices, shards(): lax.ppermute(grad_hidden, 'gx', [(dev, dev ^ hop) for dev in range(4)])  639 us
    all_gather x1, waiting for transfers between devices, shards(): lax.all_gather(up_pre, 'gx', axis=0, tiled=True)  458 us
    all_gather x1, waiting for transfers between devices, shards(): cotangent_all = lax.all_gather(cotangent, 'gy', axis=0, tiled=True)  38.8 us
    unnamed x5, local copies, waits for them, and re-layouts  37.2 us
  transfers between devices with their start and end apart: 8, of which 5 were waited for; matrix products, arithmetic and copies ran while one was open for 13% of the time, Pallas kernels for 0%

profile of v1, /device:TPU:0, one launch (start us, length us, event | category | flops | bytes accessed | tf_op | source)
XLA Modules:
  0.0 1386.5 jit_solution(9120587338531507366)
XLA Ops:
  8.0 0.7 all-gather.6.cloned.1.call-update
  8.8 38.8 %all-gather.6.cloned.1.call-done = bf16[1024,2048]{1,0:T(8,128)(2,1)} async-done(((bf16[256,2048]{1,0:T(8,128)(2,1)}), bf16[1024,2048]{1,0:T(8,128)(2,1)}) %all-gather.6.cloned.1.call-update) | async-done | bytes 4194320 | tf_op jit(solution)/shard_map/all_gather | solution.py:36
  47.6 22.5 %fusion.16 = f32[1024,3328]{1,0:T(8,128)} fusion(bf16[1024,2048]{1,0:T(8,128)(2,1)} %all-gather.6.cloned.1.call-done, bf16[3328,2048]{1,0:T(8,128)(2,1)} %param.13), kind=kOutput, calls=%fused_computation.24 | convolution fusion | flops 13958643712 | bytes 31457280 | tf_op jit(solution)/shard_map/dot_general | solution.py:41
  70.2 1.5 collective-permute-start
  71.7 0.0 all-gather.8.cloned.1.call-start
  71.7 403.3 %collective-permute-done = f32[1024,3328]{1,0:T(8,128)} collective-permute-done((f32[1024,3328]{1,0:T(8,128)}, f32[1024,3328]{1,0:T(8,128)}, u32[]{:S(2)}, u32[]{:S(2)}) %collective-permute-start) | collective-permute-done | bytes 13631520 | tf_op jit(solution)/shard_map/ppermute | solution.py:46
  475.0 14.9 %add.17 = f32[1024,3328]{1,0:T(8,128)} add(f32[1024,3328]{1,0:T(8,128)} %fusion.16, f32[1024,3328]{1,0:T(8,128)} %collective-permute-done) | non-fusion elementwise | flops 3407872 | bytes 40894464 | tf_op jit(solution)/shard_map/add | solution.py:46
  489.9 2.4 collective-permute-start.1
  492.4 0.5 all-gather.14.cloned.1.call-update
  492.9 0.3 reduce-scatter.2.cloned.1.call-start
  493.3 457.6 %all-gather.8.cloned.1.call-done = bf16[1024,3328]{1,0:T(8,128)(2,1)} async-done(((bf16[256,3328]{1,0:T(8,128)(2,1)}), bf16[1024,3328]{1,0:T(8,128)(2,1)}) %all-gather.8.cloned.1.call-update) | async-done | bytes 6815760 | tf_op jit(solution)/shard_map/all_gather | solution.py:39
  950.9 236.1 %collective-permute-done.1 = f32[1024,3328]{1,0:T(8,128)} collective-permute-done((f32[1024,3328]{1,0:T(8,128)}, f32[1024,3328]{1,0:T(8,128)}, u32[]{:S(2)}, u32[]{:S(2)}) %collective-permute-start.1) | collective-permute-done | bytes 13631520 | tf_op jit(solution)/shard_map/ppermute | solution.py:46
  1187.0 17.1 %fusion.9 = (bf16[1024,3328]{1,0:T(8,128)(2,1)S(1)}, bf16[1024,3328]{1,0:T(8,128)(2,1)}) fusion(bf16[1024,3328]{1,0:T(8,128)(2,1)} %all-gather.10.cloned.1.call-done, f32[1024,3328]{1,0:T(8,128)} %add.17, f32[1024,3328]{1,0:T(8,128)} %collective-permute-done.1, bf16[1024,3328]{1,0:T(8,128)(2,1)} %all-gather.8.cloned.1.call-done), kind=kLoop, calls=%fused_computation.18 | loop fusion | flops 54525952 | bytes 54525952 | tf_op jit(solution)/shard_map/convert_element_type | solution.py:18
  1204.1 20.6 %fusion.17 = f32[1024,2048]{1,0:T(8,128)} fusion(bf16[1024,3328]{1,0:T(8,128)(2,1)S(1)} %get-tuple-element.8, bf16[2048,3328]{1,0:T(8,128)(2,1)} %param.12), kind=kOutput, calls=%fused_computation.25 | convolution fusion | flops 13958643712 | bytes 28835840 | tf_op jit(solution)/shard_map/dot_general | solution.py:28
  1224.7 22.6 %fusion.15 = f32[1024,2048]{1,0:T(8,128)} fusion(f32[1024,2048]{1,0:T(8,128)} %fusion.17, bf16[1024,3328]{1,0:T(8,128)(2,1)} %get-tuple-element.9, bf16[2048,3328]{1,0:T(8,128)(2,1)} %param.11), kind=kOutput, calls=%fused_computation.23 | convolution fusion | flops 13960740864 | bytes 37224448 | tf_op jit(solution)/shard_map/dot_general | solution.py:25
  1247.3 0.6 all-gather.12.cloned.1.call-start
  1247.9 23.4 %convolution_convert_fusion = bf16[3328,2048]{1,0:T(8,128)(2,1)} fusion(bf16[1024,2048]{1,0:T(8,128)(2,1)} %all-gather.6.cloned.1.call-done, bf16[1024,3328]{1,0:T(8,128)(2,1)} %all-gather.8.cloned.1.call-done, bf16[1024,3328]{1,0:T(8,128)(2,1)} %all-gather.10.cloned.1.call-done), kind=kOutput, calls=%fused_computation.6 | convolution fusion | flops 13992722432 | bytes 31457280 | tf_op jit(solution)/shard_map/dot_general | solution.py:50
  1271.3 21.6 %fusion.10 = bf16[2048,3328]{0,1:T(8,128)(2,1)} fusion(bf16[1024,3328]{1,0:T(8,128)(2,1)} %get-tuple-element.9, bf16[1024,2048]{1,0:T(8,128)(2,1)} %all-gather.14.cloned.1.call-done), kind=kOutput, calls=%fused_computation.19 | convolution fusion | flops 13965459456 | bytes 24641536 | tf_op jit(solution)/shard_map/dot_general | solution.py:54
  1292.9 25.9 %reduce-scatter.2.cloned.1.call-done = f32[128,2048]{1,0:T(8,128)} async-done(((f32[1024,2048]{1,0:T(8,128)}), f32[128,2048]{1,0:T(8,128)}) %reduce-scatter.2.cloned.1.call-update) | async-done | bytes 1048592 | tf_op jit(solution)/shard_map/reduce_scatter | solution.py:59
  1318.7 2.1 convert_element_type.37
  1320.8 20.9 %fusion.11 = bf16[2048,3328]{0,1:T(8,128)(2,1)} fusion(bf16[1024,3328]{1,0:T(8,128)(2,1)} %copy-done, bf16[1024,2048]{1,0:T(8,128)(2,1)} %all-gather.14.cloned.1.call-done), kind=kOutput, calls=%fused_computation.20 | convolution fusion | flops 13965459456 | bytes 24641536 | tf_op jit(solution)/shard_map/dot_general | solution.py:55
  1341.8 17.4 %copy.11 = bf16[2048,3328]{1,0:T(8,128)(2,1)} copy(bf16[2048,3328]{0,1:T(8,128)(2,1)} %fusion.10) | data formatting | bytes 27262976
  1359.2 17.4 %copy.12 = bf16[2048,3328]{1,0:T(8,128)(2,1)} copy(bf16[2048,3328]{0,1:T(8,128)(2,1)} %fusion.11) | data formatting | bytes 27262976
  1376.7 2.3 copy.14
  (12 shorter events, 0.2 us)
Async XLA Ops:
  8.0 39.6 %all-gather.6.cloned.1.call-start = ((), (), s32[]{:S(2)}) async-start(), calls=%async_computation.1 | async-start | bytes 5242880 | tf_op jit(solution)/shard_map/all_gather | solution.py:36
  8.7 484.5 %all-gather.10.cloned.1.call-start = ((), (), s32[]{:S(2)}) async-start(), calls=%async_computation.3 | async-start | bytes 8519680 | tf_op jit(solution)/shard_map/all_gather | solution.py:38
  70.2 404.8 %collective-permute-start = (f32[1024,3328]{1,0:T(8,128)}, f32[1024,3328]{1,0:T(8,128)}, u32[]{:S(2)}, u32[]{:S(2)}) collective-permute-start(f32[1024,3328]{1,0:T(8,128)} %fusion.16), channel_id=1, source_target_pairs={{0,8},{8,0},{16,24},{24,16},{1,9},{9,1},{17,25},{25,17},{2,10},{10... | collective-permute-start | bytes 40894472 | tf_op jit(solution)/shard_map/ppermute | solution.py:46
  71.7 879.2 %all-gather.8.cloned.1.call-start = ((), (), s32[]{:S(2)}) async-start(), calls=%async_computation.2 | async-start | bytes 8519680 | tf_op jit(solution)/shard_map/all_gather | solution.py:39
  489.9 697.1 %collective-permute-start.1 = (f32[1024,3328]{1,0:T(8,128)}, f32[1024,3328]{1,0:T(8,128)}, u32[]{:S(2)}, u32[]{:S(2)}) collective-permute-start(f32[1024,3328]{1,0:T(8,128)} %add.17), channel_id=1, source_target_pairs={{0,16},{8,24},{16,0},{24,8},{1,17},{9,25},{17,1},{25,9},{2,18},{10... | collective-permute-start | bytes 40894472 | tf_op jit(solution)/shard_map/ppermute | solution.py:46
  492.3 779.0 %all-gather.14.cloned.1.call-start = ((), (), s32[]{:S(2)}) async-start(), calls=%async_computation.6 | async-start | bytes 5242880 | tf_op jit(solution)/shard_map/all_gather | solution.py:53
  492.9 825.8 %reduce-scatter.2.cloned.1.call-start = ((), (), s32[]{:S(2)}) async-start(), calls=%async_computation.4 | async-start | bytes 9437184 | tf_op jit(solution)/shard_map/reduce_scatter | solution.py:59
  1204.1 20.6 %copy-start = (bf16[1024,3328]{1,0:T(8,128)(2,1)}, bf16[1024,3328]{1,0:T(8,128)(2,1)S(1)}, u32[]{:S(2)}) copy-start(bf16[1024,3328]{1,0:T(8,128)(2,1)S(1)} %get-tuple-element.8) | copy-start | bytes 20447236
  1247.3 129.3 %all-gather.12.cloned.1.call-start = ((), (), s32[]{:S(2)}) async-start(), calls=%async_computation.5 | async-start | bytes 1572864 | tf_op jit(solution)/shard_map/all_gather | solution.py:65
Sparse Core Ops, SparseCore 0:
  10.4 37.1 all-gather.5
  1247.4 71.2 reduce-scatter.1
  1320.9 21.2 all-gather.11
Sparse Core Ops, SparseCore 1:
  71.7 227.8 all-gather.9
  492.4 458.4 all-gather.7
  952.4 33.3 all-gather.13
